TPU v7x, 256 devices: a whole 4x4x8 slice. The times are simulated.
256 devices in a mesh: section: 2 (over core), grp: 4 (over x), dev: 32 (over y, z).
Axes of the slice: x: 4, y: 4, z: 8, core: 2. Of those that a mesh axis runs over, the one named last changes fastest.
Arguments:
- frames: bfloat16 [4, 512, 512, 256], P('grp', 'dev', 'section'), may hold values from -6 to 6
- templates: bfloat16 [8192, 256], P('dev'), may hold values from -0.375 to 0.375
- pair_block: int32 [2, 4, 256], P('section', 'grp', 'dev'), may hold values from 0 to 63
- pair_tile: int32 [2, 4, 256], P('section', 'grp', 'dev'), may hold values from 0 to 3
- pair_count: int32 [2, 4, 32], P('section', 'grp', 'dev'), may hold values from 1 to 8, 128 in all within a row
- owner_order: int32 [8192], replicated, may hold values from 0 to 8191, each once
Outputs:
- quantities: float32 [4, 8192], P('grp', 'dev')
Inputs may be any that keep to these rules, and one draw needn't show every extreme that they name: `pair_count`: each device's count of live slots; the counts of one section half and run sum to half of all slots there, and one of them is 8. `owner_order`: A permutation of the precursors.
All inputs are finite; a program needn't handle non-finite values.
Results may differ from a plain program's by a relative error of at most 0.00037.
Values may be sent and summed in bfloat16 or wider, within the bound.
A program may use at most 64 MiB of HBM per device.

v0:
```python
import math
import jax
import jax.numpy as jnp
from jax import lax
from jax.sharding import PartitionSpec as P

MOB = 512
SCALES = 6
RAD = 4
TM = 64
PB = 128
PREC = 8192
retention_spread = 2.0


def extended(cells, sides, width):
    for axis, dim in sides:
        count = lax.axis_size(axis)
        ends = count - 1
        head = lax.slice_in_dim(cells, 0, width, axis=dim)
        tail = lax.slice_in_dim(cells, cells.shape[dim] - width, cells.shape[dim], axis=dim)
        cells = jnp.concatenate(
            [
                lax.ppermute(tail, axis, [(i, (i + 1) % count) for i in range(ends)]),
                cells,
                lax.ppermute(head, axis, [((i + 1) % count, i) for i in range(ends)]),
            ],
            axis=dim,
        )
    return cells


def retention_weights():
    bell_values = [
        math.exp(-0.5 * (offset / retention_spread) ** 2) for offset in range(-RAD, RAD + 1)
    ]
    bell_total = sum(bell_values)
    return [weight_value / bell_total for weight_value in bell_values]


def mobility_kernels(row_start, row_count):
    row_place = (row_start + jnp.arange(row_count, dtype=jnp.int32)).astype(jnp.float32)
    col_place = jnp.arange(MOB, dtype=jnp.int32).astype(jnp.float32)
    distance = row_place[:, None] - col_place[None, :]
    tables = []
    for level in range(SCALES):
        spread_scans = 2.0**level
        scaled = distance / spread_scans
        tables.append(
            (1.0 - scaled * scaled)
            * jnp.exp(-0.5 * scaled * scaled)
            / math.sqrt(0.75 * math.sqrt(math.pi) * spread_scans)
        )
    return jnp.stack(tables).astype(jnp.bfloat16)


def on_device(frames, templates, pair_block, pair_tile, pair_count, owner_order):
    section_index = lax.axis_index("section")
    weights = retention_weights()
    count_frames = frames.shape[1]
    mob_local = frames.shape[2]
    channels = frames.shape[3]
    framed = extended(frames, (("dev", 1),), RAD)
    padded = framed.astype(jnp.float32)
    smoothed = weights[0] * padded[:, 0:count_frames]
    for offset in range(1, 2 * RAD + 1):
        smoothed = smoothed + weights[offset] * padded[:, offset : offset + count_frames]
    smoothed = smoothed.astype(jnp.bfloat16)
    gathered = lax.all_gather(smoothed, "section", axis=2, tiled=True)
    kernels = mobility_kernels(section_index * mob_local, mob_local)
    wavelet_stack = jnp.einsum(
        "smn,fnc->smfc", kernels, gathered[0], preferred_element_type=jnp.float32
    ).astype(jnp.bfloat16)
    template_panel = lax.all_gather(templates, "dev", axis=0, tiled=True)
    blocks = template_panel.shape[0] // PB
    live_pairs = pair_count[0, 0, 0]
    block_ids = pair_block[0, 0]
    tile_ids = pair_tile[0, 0]

    def visit_pair(slot_index, totals):
        block_id = block_ids[slot_index]
        tile_id = tile_ids[slot_index]
        tile_cells = lax.dynamic_slice_in_dim(wavelet_stack, tile_id * TM, TM, 1).reshape(
            -1, channels
        )
        block_rows = lax.dynamic_slice_in_dim(template_panel, block_id * PB, PB, 0)
        scores = jnp.dot(tile_cells, block_rows.T, preferred_element_type=jnp.float32)
        response = jnp.mean(jnp.maximum(scores, 0.0), axis=0)
        block_hit = (jnp.arange(blocks, dtype=jnp.int32) == block_id).astype(jnp.float32)
        return totals + block_hit[:, None] * response[None, :]

    totals = lax.fori_loop(0, live_pairs, visit_pair, jnp.zeros((blocks, PB), jnp.float32))
    placed = jnp.zeros((PREC,), jnp.float32).at[owner_order].set(totals.reshape(-1))[None]
    summed = lax.psum(placed, "section")
    owned = lax.psum_scatter(summed, "dev", scatter_dimension=1, tiled=True)
    run_count = lax.axis_size("grp")
    run_mask = (jnp.arange(run_count, dtype=jnp.int32) == lax.axis_index("grp")).astype(jnp.float32)
    run_totals = lax.psum(run_mask * jnp.sum(owned), ("grp", "dev"))
    own_total = jnp.sum(run_totals * run_mask)
    factor = jnp.mean(run_totals) / own_total
    return owned * factor


def solution(mesh):
    placed = (
        P("grp", "dev", "section", None),
        P("dev", None),
        P("section", "grp", "dev"),
        P("section", "grp", "dev"),
        P("section", "grp", "dev"),
        P(),
    )
    return jax.shard_map(
        on_device, mesh=mesh, in_specs=placed, out_specs=P("grp", "dev"), check_vma=False
    )
```

profile of v0, /device:TPU:0, one launch (start us, length us, event | category | flops | bytes accessed | tf_op | source)
XLA Modules:
  0.0 833.9 jit_solution(16655650894832102042)
XLA Ops:
  6.5 1.3 fusion.63
  7.8 2.1 collective-permute-start
  9.9 1.3 collective-permute-start.1
  11.2 9.8 %collective-permute-done = bf16[1,4,256,256]{3,2,1,0:T(8,128)(2,1)S(1)} collective-permute-done((bf16[1,4,256,256]{3,2,1,0:T(8,128)(2,1)S(1)}, bf16[1,4,256,256]{3,2,1,0:T(8,128)(2,1)S(1)}, u32[]{:S(2)}, u32[]{:S(2)}) %collective-permute-start) | collective-permute-done | bytes 524320 | tf_op jit(solution)/shard_map/ppermute | solution.py:24
  21.1 4.3 collective-permute-done.1
  25.4 2.1 maximum_convert_fusion
  27.4 5.7 fusion.4
  33.2 0.7 all-gather.5.cloned.1.call-update
  35.6 19.7 %all-gather.3.cloned.1.call-done = bf16[1,16,512,256]{3,2,1,0:T(8,128)(2,1)} async-done(((bf16[1,16,256,256]{3,2,1,0:T(8,128)(2,1)}), bf16[1,16,512,256]{3,2,1,0:T(8,128)(2,1)}) %all-gather.3.cloned.1.call-update) | async-done | bytes 4194320 | tf_op jit(solution)/shard_map/all_gather | solution.py:69
  55.2 11.7 %convolution_convert_fusion = bf16[6,256,16,256]{3,1,2,0:T(8,128)(2,1)} fusion(bf16[1,16,512,256]{3,2,1,0:T(8,128)(2,1)} %all-gather.3.cloned.1.call-done, bf16[6,256,512]{2,1,0:T(8,128)(2,1)S(1)} %fusion.58), kind=kOutput, calls=%fused_computation.9 | convolution fusion | flops 6448742400 | bytes 18350080 | tf_op jit(solution)/shard_map/smn,fnc->smfc/dot_general | solution.py:71
  66.9 73.7 %all-gather.5.cloned.1.call-done = bf16[8192,256]{1,0:T(8,128)(2,1)} async-done(((bf16[256,256]{1,0:T(8,128)(2,1)}), bf16[8192,256]{1,0:T(8,128)(2,1)}) %all-gather.5.cloned.1.call-update) | async-done | bytes 4194320 | tf_op jit(solution)/shard_map/all_gather | solution.py:74
  140.7 10.7 %while.10 = (s32[]{:T(128)}, f32[64,128]{1,0:T(8,128)S(1)}, s32[]{:T(128)}, s32[8]{0:T(128)S(1)}, s32[8]{0:T(128)S(1)}, /*index=5*/bf16[6,256,16,256]{3,1,2,0:T(...) while((s32[]{:T(128)}, f32[64,128]{1,0:T(8,128)S(1)}, ...), condition=%wide.region_2.0_spmd, body=%wide.region_0.0_spmd.sunk | while | flops 404242560 | bytes 15862567 | solution.py:92
  142.5 2.3 constant_dynamic-slice_fusion.2
  144.8 1.9 copy.14
  147.9 2.2 fusion.70
  151.4 30.5 %scatter_custom_fusion = f32[8192]{0:T(1024)S(1)} fusion(s32[8192]{0:T(1024)S(1)} %compare_select_fusion, f32[8192]{0:T(1024)S(1)} %bitcast.30, f32[]{:T(128)} %constant.32.clone.1), kind=kCustom, calls=%fused_computation.91 | custom fusion | bytes 32772 | tf_op jit(solution)/shard_map/scatter | solution.py:93
  181.9 2.6 copy.10
  184.6 288.7 %reduce-scatter.4.cloned.1.call-done = f32[256,1]{1,0:T(8,128)} async-done(((f32[8192,1]{1,0:T(8,128)}), f32[256,1]{1,0:T(8,128)}) %reduce-scatter.4.cloned.1.call-update) | async-done | bytes 1040
  473.2 1.0 copy.11
  474.2 2.5 psum.16
  476.7 0.6 reduce_sum.36
  477.3 0.6 compare_select_fusion.2
  477.9 346.8 %psum.15 = f32[4]{0:T(128)S(1)} all-reduce(f32[4]{0:T(128)S(1)} %compare_select_fusion.2), channel_id=1, replica_groups=mesh['section'=2,'grp'=4,'dev'=32] {'grp','dev'}, use_global_device_ids=true, to_apply=%region_7.0 | all-reduce | flops 4 | bytes 32 | tf_op jit(solution)/shard_map/psum | solution.py:98
  824.8 0.7 fusion.62
  (27 shorter events, 4.0 us)
Async XLA Ops:
  6.5 48.7 %all-gather.3.cloned.1.call-start = ((), (), s32[]{:S(2)}) async-start(), calls=%async_computation.1 | async-start | bytes 6291456 | tf_op jit(solution)/shard_map/all_gather | solution.py:69
  7.8 13.3 %collective-permute-start = (bf16[1,4,256,256]{3,2,1,0:T(8,128)(2,1)S(1)}, bf16[1,4,256,256]{3,2,1,0:T(8,128)(2,1)S(1)}, u32[]{:S(2)}, u32[]{:S(2)}) collective-permute-start(bf16[1,4,256,256]{3,2,1,0:T(8,128)(2,1)S(1)} %get-tuple-element.74), channel_id=1, source_target_pairs={{0,1},{1,2},{2,3},{3,4},{4,5},{5,6},{6,7},{7,8},{8,9},{9,10},{10,1... | collective-permute-start | bytes 1572872 | tf_op jit(solution)/shard_map/ppermute | solution.py:24
  9.9 15.4 %collective-permute-start.1 = (bf16[1,4,256,256]{3,2,1,0:T(8,128)(2,1)S(1)}, bf16[1,4,256,256]{3,2,1,0:T(8,128)(2,1)S(1)}, u32[]{:S(2)}, u32[]{:S(2)}) collective-permute-start(bf16[1,4,256,256]{3,2,1,0:T(8,128)(2,1)S(1)} %get-tuple-element.75), channel_id=1, source_target_pairs={{1,0},{2,1},{3,2},{4,3},{5,4},{6,5},{7,6},{8,7},{9,8},{10,9},{11,1... | collective-permute-start | bytes 1572872 | tf_op jit(solution)/shard_map/ppermute | solution.py:26
  27.4 6.6 copy-start
  33.2 107.5 %all-gather.5.cloned.1.call-start = ((), (), s32[]{:S(2)}) async-start(), calls=%async_computation.2 | async-start | bytes 4325376 | tf_op jit(solution)/shard_map/all_gather | solution.py:74
  33.9 439.3 %reduce-scatter.4.cloned.1.call-start = ((), (), s32[]{:S(2)}) async-start(), calls=%async_computation.3 | async-start | bytes 4325376
  35.5 105.1 %copy-start.1 = (s32[1,1,8]{2,1,0:T(1,128)S(1)}, s32[1,1,8]{2,1,0:T(1,128)}, u32[]{:S(2)}) copy-start(s32[1,1,8]{2,1,0:T(1,128)} %param.10) | copy-start | bytes 100
  35.6 105.1 %copy-start.2 = (s32[1,1,8]{2,1,0:T(1,128)S(1)}, s32[1,1,8]{2,1,0:T(1,128)}, u32[]{:S(2)}) copy-start(s32[1,1,8]{2,1,0:T(1,128)} %param.11) | copy-start | bytes 100
Sparse Core Ops, SparseCore 0:
  33.3 21.9 all-gather.2
  57.8 82.8 all-gather.4
  184.7 288.5 reduce-scatter.3
where the time goes:
time: 835 us; the launch traced here: 834 us
  waiting for transfers between devices  397 us (48%)
  blocking collectives  349 us (42%)
  local copies, waits for them, and re-layouts  40.7 us (5%)
  between operations  14.6 us (2%)
  matrix products  13.9 us (2%)
  other arithmetic  12.4 us (1%)
    psum x1, blocking collectives, on_device(): run_totals = lax.psum(run_mask * jnp.sum(owned), ('grp', 'dev'))  347 us
    unnamed x4, waiting for transfers between devices  289 us
    all_gather x1, waiting for transfers between devices, on_device(): template_panel = lax.all_gather(templates, 'dev', axis=0, tiled=True)  73.7 us
    scatter x1, local copies, waits for them, and re-layouts, on_device(): jnp.zeros((PREC,), jnp.float32).at[owner_order].set(totals.reshape(-1))  30.5 us
    all_gather x1, waiting for transfers between devices, on_device(): gathered = lax.all_gather(smoothed, 'section', axis=2, tiled=True)  19.7 us
  transfers between devices with their start and end apart: 5, of which 5 were waited for; matrix products, arithmetic and copies ran while one was open for 2% of the time, Pallas kernels for 0%

commit v1 on v0

--- a/solution.py
+++ b/solution.py
@@ -95,7 +95,7 @@
     owned = lax.psum_scatter(summed, "dev", scatter_dimension=1, tiled=True)
     run_count = lax.axis_size("grp")
     run_mask = (jnp.arange(run_count, dtype=jnp.int32) == lax.axis_index("grp")).astype(jnp.float32)
-    run_totals = lax.psum(run_mask * jnp.sum(owned), ("grp", "dev"))
+    run_totals = lax.psum(lax.psum(run_mask * jnp.sum(owned), "dev"), "grp")
     own_total = jnp.sum(run_totals * run_mask)
     factor = jnp.mean(run_totals) / own_total
     return owned * factor

time: 835 us -> 571 us (0.68)
  blocking collectives: 349 us -> 85.1 us
    psum x1 -> x2, blocking collectives: 347 us -> 82.6 us  [on_device(): run_totals = lax.psum(lax.psum(run_mask * jnp.sum(owned), 'dev'), 'grp')]
where the time goes in v1:
time: 571 us; the launch traced here: 570 us
  waiting for transfers between devices  397 us (70%)
  blocking collectives  85.1 us (15%)
  local copies, waits for them, and re-layouts  40.7 us (7%)
  between operations  14.6 us (3%)
  matrix products  13.9 us (2%)
  other arithmetic  12.4 us (2%)
    unnamed x4, waiting for transfers between devices  289 us
    psum x2, blocking collectives, on_device(): run_totals = lax.psum(lax.psum(run_mask * jnp.sum(owned), 'dev'), 'grp')  82.6 us
    all_gather x1, waiting for transfers between devices, on_device(): template_panel = lax.all_gather(templates, 'dev', axis=0, tiled=True)  73.7 us
    scatter x1, local copies, waits for them, and re-layouts, on_device(): jnp.zeros((PREC,), jnp.float32).at[owner_order].set(totals.reshape(-1))  30.5 us
    all_gather x1, waiting for transfers between devices, on_device(): gathered = lax.all_gather(smoothed, 'section', axis=2, tiled=True)  19.7 us
    dot_general x1, matrix products, on_device(): jnp.einsum('smn,fnc->smfc', kernels, gathered[0], preferred_element_type=...  11.7 us
  transfers between devices with their start and end apart: 5, of which 5 were waited for; matrix products, arithmetic and copies ran while one was open for 2% of the time, Pallas kernels for 0%

profile of v1, /device:TPU:0, one launch (start us, length us, event | category | flops | bytes accessed | tf_op | source)
XLA Modules:
  0.0 569.7 jit_solution(9671011822080812713)
XLA Ops:
  6.5 1.3 fusion.63
  7.8 2.1 collective-permute-start
  9.9 1.3 collective-permute-start.1
  11.2 9.8 %collective-permute-done = bf16[1,4,256,256]{3,2,1,0:T(8,128)(2,1)S(1)} collective-permute-done((bf16[1,4,256,256]{3,2,1,0:T(8,128)(2,1)S(1)}, bf16[1,4,256,256]{3,2,1,0:T(8,128)(2,1)S(1)}, u32[]{:S(2)}, u32[]{:S(2)}) %collective-permute-start) | collective-permute-done | bytes 524320 | tf_op jit(solution)/shard_map/ppermute | solution.py:24
  21.1 4.3 collective-permute-done.1
  25.4 2.1 maximum_convert_fusion
  27.4 5.7 %fusion.4 = bf16[1,16,256,256]{3,2,1,0:T(8,128)(2,1)} fusion(f32[1,24,256,256]{3,2,1,0:T(8,128)S(1)} %maximum_convert_fusion), kind=kLoop, calls=%fused_computation.12 | loop fusion | flops 18874368 | bytes 39845888 | tf_op jit(solution)/shard_map/convert_element_type | solution.py:68
  33.2 0.7 all-gather.5.cloned.1.call-update
  35.6 19.7 %all-gather.3.cloned.1.call-done = bf16[1,16,512,256]{3,2,1,0:T(8,128)(2,1)} async-done(((bf16[1,16,256,256]{3,2,1,0:T(8,128)(2,1)}), bf16[1,16,512,256]{3,2,1,0:T(8,128)(2,1)}) %all-gather.3.cloned.1.call-update) | async-done | bytes 4194320 | tf_op jit(solution)/shard_map/all_gather | solution.py:69
  55.2 11.7 %convolution_convert_fusion = bf16[6,256,16,256]{3,1,2,0:T(8,128)(2,1)} fusion(bf16[1,16,512,256]{3,2,1,0:T(8,128)(2,1)} %all-gather.3.cloned.1.call-done, bf16[6,256,512]{2,1,0:T(8,128)(2,1)S(1)} %fusion.58), kind=kOutput, calls=%fused_computation.9 | convolution fusion | flops 6448742400 | bytes 18350080 | tf_op jit(solution)/shard_map/smn,fnc->smfc/dot_general | solution.py:71
  66.9 73.7 %all-gather.5.cloned.1.call-done = bf16[8192,256]{1,0:T(8,128)(2,1)} async-done(((bf16[256,256]{1,0:T(8,128)(2,1)}), bf16[8192,256]{1,0:T(8,128)(2,1)}) %all-gather.5.cloned.1.call-update) | async-done | bytes 4194320 | tf_op jit(solution)/shard_map/all_gather | solution.py:74
  140.7 10.7 %while.10 = (s32[]{:T(128)}, f32[64,128]{1,0:T(8,128)S(1)}, s32[]{:T(128)}, s32[8]{0:T(128)S(1)}, s32[8]{0:T(128)S(1)}, /*index=5*/bf16[6,256,16,256]{3,1,2,0:T(...) while((s32[]{:T(128)}, f32[64,128]{1,0:T(8,128)S(1)}, ...), condition=%wide.region_2.0_spmd, body=%wide.region_0.0_spmd.sunk | while | flops 404242560 | bytes 15862567 | solution.py:92
  142.5 2.3 constant_dynamic-slice_fusion.2
  144.8 1.9 copy.14
  147.9 2.2 fusion.70
  151.4 30.5 %scatter_custom_fusion = f32[8192]{0:T(1024)S(1)} fusion(s32[8192]{0:T(1024)S(1)} %compare_select_fusion, f32[8192]{0:T(1024)S(1)} %bitcast.30, f32[]{:T(128)} %constant.32.clone.1), kind=kCustom, calls=%fused_computation.91 | custom fusion | bytes 32772 | tf_op jit(solution)/shard_map/scatter | solution.py:93
  181.9 2.6 copy.10
  184.6 288.7 %reduce-scatter.4.cloned.1.call-done = f32[256,1]{1,0:T(8,128)} async-done(((f32[8192,1]{1,0:T(8,128)}), f32[256,1]{1,0:T(8,128)}) %reduce-scatter.4.cloned.1.call-update) | async-done | bytes 1040
  473.2 1.0 copy.11
  474.2 2.5 psum.24
  477.3 0.6 compare_select_fusion.2
  477.9 72.2 %psum.22 = f32[4]{0:T(128)S(1)} all-reduce(f32[4]{0:T(128)S(1)} %compare_select_fusion.2), channel_id=1, replica_groups=mesh['section'=2,'grp'=4,'dev'=32] {'dev'}, use_global_device_ids=true, to_apply=%region_7.0 | all-reduce | flops 4 | bytes 32 | tf_op jit(solution)/shard_map/psum | solution.py:98
  550.1 10.4 %psum.23 = f32[4]{0:T(128)S(1)} all-reduce(f32[4]{0:T(128)S(1)} %psum.22), channel_id=1, replica_groups=mesh['section'=2,'grp'=4,'dev'=32] {'grp'}, use_global_device_ids=true, to_apply=%region_8.0 | all-reduce | flops 4 | bytes 32 | tf_op jit(solution)/shard_map/psum | solution.py:98
  560.5 0.7 fusion.62
  (28 shorter events, 4.6 us)
Async XLA Ops:
  6.5 48.7 %all-gather.3.cloned.1.call-start = ((), (), s32[]{:S(2)}) async-start(), calls=%async_computation.1 | async-start | bytes 6291456 | tf_op jit(solution)/shard_map/all_gather | solution.py:69
  7.8 13.3 %collective-permute-start = (bf16[1,4,256,256]{3,2,1,0:T(8,128)(2,1)S(1)}, bf16[1,4,256,256]{3,2,1,0:T(8,128)(2,1)S(1)}, u32[]{:S(2)}, u32[]{:S(2)}) collective-permute-start(bf16[1,4,256,256]{3,2,1,0:T(8,128)(2,1)S(1)} %get-tuple-element.74), channel_id=1, source_target_pairs={{0,1},{1,2},{2,3},{3,4},{4,5},{5,6},{6,7},{7,8},{8,9},{9,10},{10,1... | collective-permute-start | bytes 1572872 | tf_op jit(solution)/shard_map/ppermute | solution.py:24
  9.9 15.4 %collective-permute-start.1 = (bf16[1,4,256,256]{3,2,1,0:T(8,128)(2,1)S(1)}, bf16[1,4,256,256]{3,2,1,0:T(8,128)(2,1)S(1)}, u32[]{:S(2)}, u32[]{:S(2)}) collective-permute-start(bf16[1,4,256,256]{3,2,1,0:T(8,128)(2,1)S(1)} %get-tuple-element.75), channel_id=1, source_target_pairs={{1,0},{2,1},{3,2},{4,3},{5,4},{6,5},{7,6},{8,7},{9,8},{10,9},{11,1... | collective-permute-start | bytes 1572872 | tf_op jit(solution)/shard_map/ppermute | solution.py:26
  27.4 6.6 %copy-start = (s32[8192]{0:T(1024)S(1)}, s32[8192]{0:T(1024)}, u32[]{:S(2)}) copy-start(s32[8192]{0:T(1024)} %param.13) | copy-start | bytes 98308
  33.2 107.5 %all-gather.5.cloned.1.call-start = ((), (), s32[]{:S(2)}) async-start(), calls=%async_computation.2 | async-start | bytes 4325376 | tf_op jit(solution)/shard_map/all_gather | solution.py:74
  33.9 439.3 %reduce-scatter.4.cloned.1.call-start = ((), (), s32[]{:S(2)}) async-start(), calls=%async_computation.3 | async-start | bytes 4325376
  35.5 105.1 %copy-start.1 = (s32[1,1,8]{2,1,0:T(1,128)S(1)}, s32[1,1,8]{2,1,0:T(1,128)}, u32[]{:S(2)}) copy-start(s32[1,1,8]{2,1,0:T(1,128)} %param.10) | copy-start | bytes 100
  35.6 105.1 %copy-start.2 = (s32[1,1,8]{2,1,0:T(1,128)S(1)}, s32[1,1,8]{2,1,0:T(1,128)}, u32[]{:S(2)}) copy-start(s32[1,1,8]{2,1,0:T(1,128)} %param.11) | copy-start | bytes 100
Sparse Core Ops, SparseCore 0:
  33.3 21.9 all-gather.2
  57.8 82.8 all-gather.4
  184.7 288.5 reduce-scatter.3

commit v2 on v0

--- a/solution.py
+++ b/solution.py
@@ -66,7 +66,9 @@
     for offset in range(1, 2 * RAD + 1):
         smoothed = smoothed + weights[offset] * padded[:, offset : offset + count_frames]
     smoothed = smoothed.astype(jnp.bfloat16)
-    gathered = lax.all_gather(smoothed, "section", axis=2, tiled=True)
+    gathered = jnp.concatenate(
+        lax.all_to_all(jnp.stack([smoothed] * lax.axis_size("section")), "section", 0, 0), axis=2
+    )
     kernels = mobility_kernels(section_index * mob_local, mob_local)
     wavelet_stack = jnp.einsum(
         "smn,fnc->smfc", kernels, gathered[0], preferred_element_type=jnp.float32

time: 835 us -> 789 us (0.945)
  waiting for transfers between devices: 397 us -> 340 us
    all_gather x1, waiting for transfers between devices: 73.7 us -> 41.8 us  [on_device(): template_panel = lax.all_gather(templates, 'dev', axis=0, tiled=True)]
    all_gather x1 -> x0, waiting for transfers between devices: 19.7 us -> none  [on_device(): gathered = lax.all_gather(smoothed, 'section', axis=2, tiled=True)]
    unnamed x4 -> x3, waiting for transfers between devices: 289 us -> 289 us
  transfers between devices with their start and end apart: 5 -> 4, of which waited for: 5 -> 4; matrix products, arithmetic and copies ran while one was open for 2% -> 3% of each run, Pallas kernels for 0% -> 0%
where the time goes in v2:
time: 789 us; the launch traced here: 788 us
  blocking collectives  356 us (45%)
  waiting for transfers between devices  340 us (43%)
  local copies, waits for them, and re-layouts  42.1 us (5%)
  other arithmetic  15.2 us (2%)
  between operations  14.9 us (2%)
  matrix products  13.3 us (2%)
    psum x1, blocking collectives, on_device(): run_totals = lax.psum(run_mask * jnp.sum(owned), ('grp', 'dev'))  347 us
    unnamed x3, waiting for transfers between devices  289 us
    all_gather x1, waiting for transfers between devices, on_device(): template_panel = lax.all_gather(templates, 'dev', axis=0, tiled=True)  41.8 us
    scatter x1, local copies, waits for them, and re-layouts, on_device(): jnp.zeros((PREC,), jnp.float32).at[owner_order].set(totals.reshape(-1))  30.5 us
  transfers between devices with their start and end apart: 4, of which 4 were waited for; matrix products, arithmetic and copies ran while one was open for 3% of the time, Pallas kernels for 0%

profile of v2, /device:TPU:0, one launch (start us, length us, event | category | flops | bytes accessed | tf_op | source)
XLA Modules:
  0.0 787.7 jit_solution(16209346239658800546)
XLA Ops:
  7.3 2.3 fusion.63
  9.6 2.1 collective-permute-start
  11.7 1.3 collective-permute-start.1
  13.9 0.9 fusion.54
  14.9 1.0 fusion.55
  15.8 1.0 fusion.56
  17.6 1.0 fusion.57
  18.5 1.0 fusion.58
  19.5 3.6 collective-permute-done
  23.1 4.9 collective-permute-done.1
  28.5 4.7 fusion.12
  33.6 7.1 all_to_all.5
  41.2 11.1 %convolution_convert_fusion = bf16[6,256,16,256]{3,1,2,0:T(8,128)(2,1)} fusion(bf16[16,512,256,1]{2,1,0,3:T(8,128)(2,1)S(1)} %bitcast.34, bf16[6,256,512]{2,1,0:T(8,128)(2,1)} %fusion.58), kind=kOutput, calls=%fused_computation.9 | convolution fusion | flops 6448742400 | bytes 18350080 | tf_op jit(solution)/shard_map/smn,fnc->smfc/dot_general | solution.py:73
  52.3 41.8 %all-gather.2.cloned.1.call-done = bf16[8192,256]{1,0:T(8,128)(2,1)} async-done(((bf16[256,256]{1,0:T(8,128)(2,1)}), bf16[8192,256]{1,0:T(8,128)(2,1)}) %all-gather.2.cloned.1.call-update) | async-done | bytes 4194320 | tf_op jit(solution)/shard_map/all_gather | solution.py:76
  94.0 10.9 %while.10 = (s32[]{:T(128)}, f32[64,128]{1,0:T(8,128)S(1)}, s32[]{:T(128)}, s32[8]{0:T(128)S(1)}, s32[8]{0:T(128)S(1)}, /*index=5*/bf16[6,256,16,256]{3,1,2,0:T(...) while((s32[]{:T(128)}, f32[64,128]{1,0:T(8,128)S(1)}, ...), condition=%wide.region_2.0_spmd, body=%wide.region_0.0_spmd.sunk | while | flops 404242560 | bytes 15862567 | solution.py:94
  96.0 2.3 constant_dynamic-slice_fusion.2
  98.4 1.9 copy.16
  101.4 2.2 fusion.71
  105.0 30.5 %scatter_custom_fusion = f32[8192]{0:T(1024)S(1)} fusion(s32[8192]{0:T(1024)S(1)} %compare_select_fusion, f32[8192]{0:T(1024)S(1)} %bitcast.35, f32[]{:T(128)} %constant.32.clone.1), kind=kCustom, calls=%fused_computation.92 | custom fusion | bytes 32772 | tf_op jit(solution)/shard_map/scatter | solution.py:95
  135.4 2.6 copy.12
  138.1 288.6 %reduce-scatter.4.cloned.1.call-done = f32[256,1]{1,0:T(8,128)} async-done(((f32[8192,1]{1,0:T(8,128)}), f32[256,1]{1,0:T(8,128)}) %reduce-scatter.4.cloned.1.call-update) | async-done | bytes 1040
  426.7 1.0 copy.13
  427.7 2.5 psum.16
  431.4 346.8 %psum.15 = f32[4]{0:T(128)S(1)} all-reduce(f32[4]{0:T(128)S(1)} %compare_select_fusion.2), channel_id=1, replica_groups=mesh['section'=2,'grp'=4,'dev'=32] {'grp','dev'}, use_global_device_ids=true, to_apply=%region_7.0 | all-reduce | flops 4 | bytes 32 | tf_op jit(solution)/shard_map/psum | solution.py:100
  (27 shorter events, 8.1 us)
Async XLA Ops:
  6.5 21.5 %copy-start = (bf16[1,16,256,256]{3,2,1,0:T(8,128)(2,1)S(1)}, bf16[1,16,256,256]{3,2,1,0:T(8,128)(2,1)}, u32[]{:S(2)}) copy-start(bf16[1,16,256,256]{3,2,1,0:T(8,128)(2,1)} %param.8) | copy-start | bytes 6291460
  6.5 87.5 %all-gather.2.cloned.1.call-start = ((), (), s32[]{:S(2)}) async-start(), calls=%async_computation.2 | async-start | bytes 4325376 | tf_op jit(solution)/shard_map/all_gather | solution.py:76
  7.3 419.4 %reduce-scatter.4.cloned.1.call-start = ((), (), s32[]{:S(2)}) async-start(), calls=%async_computation.3 | async-start | bytes 4325376
  9.6 13.6 %collective-permute-start = (bf16[1,4,256,256]{3,2,1,0:T(8,128)(2,1)}, bf16[1,4,256,256]{3,2,1,0:T(8,128)(2,1)S(1)}, u32[]{:S(2)}, u32[]{:S(2)}) collective-permute-start(bf16[1,4,256,256]{3,2,1,0:T(8,128)(2,1)} %get-tuple-element.74), channel_id=1, source_target_pairs={{0,1},{1,2},{2,3},{3,4},{4,5},{5,6},{6,7},{7,8},{8,9},{9,10},{10,1... | collective-permute-start | bytes 1572872 | tf_op jit(solution)/shard_map/ppermute | solution.py:24
  11.7 16.3 %collective-permute-start.1 = (bf16[1,4,256,256]{3,2,1,0:T(8,128)(2,1)}, bf16[1,4,256,256]{3,2,1,0:T(8,128)(2,1)S(1)}, u32[]{:S(2)}, u32[]{:S(2)}) collective-permute-start(bf16[1,4,256,256]{3,2,1,0:T(8,128)(2,1)} %get-tuple-element.75), channel_id=1, source_target_pairs={{1,0},{2,1},{3,2},{4,3},{5,4},{6,5},{7,6},{8,7},{9,8},{10,9},{11,1... | collective-permute-start | bytes 1572872 | tf_op jit(solution)/shard_map/ppermute | solution.py:26
  41.2 52.9 %copy-start.1 = (s32[1,1,8]{2,1,0:T(1,128)S(1)}, s32[1,1,8]{2,1,0:T(1,128)}, u32[]{:S(2)}) copy-start(s32[1,1,8]{2,1,0:T(1,128)} %param.10) | copy-start | bytes 100
  41.2 52.9 %copy-start.2 = (s32[1,1,8]{2,1,0:T(1,128)S(1)}, s32[1,1,8]{2,1,0:T(1,128)}, u32[]{:S(2)}) copy-start(s32[1,1,8]{2,1,0:T(1,128)} %param.11) | copy-start | bytes 100
Sparse Core Ops, SparseCore 0:
  9.9 84.0 all-gather.1
  138.2 288.4 reduce-scatter.3
